TPU v7x, 32 devices: a whole 2x2x4 slice. The times are simulated.
32 devices in a mesh: ctx: 8 (over y, x, core), chan: 4 (over z).
Axes of the slice: x: 2, y: 2, z: 4, core: 2. Of those that a mesh axis runs over, the one named last changes fastest.
Arguments:
- inputs: bfloat16 [256, 4096], P('ctx', 'chan'), may hold values from -6 to 6
- gain: float32 [4096], replicated, may hold values from 0.25 to 1.75
- w_in: bfloat16 [4096, 3, 4096], P(None, None, 'chan'), may hold values from -0.09375 to 0.09375
- w_out: bfloat16 [4096, 4096], P('chan'), may hold values from -0.125 to 0.125
- history: bfloat16 [2048, 2, 4096], P('ctx', None, 'chan'), may hold values from -6 to 6
- filt_far: bfloat16 [2048, 2, 4096], P('ctx', None, 'chan'), may hold values from -0.125 to 0.125
- filt_near: bfloat16 [256, 2, 4096], P(None, None, 'chan'), may hold values from -0.125 to 0.125
Outputs:
- mixed: bfloat16 [256, 4096], P('ctx', 'chan')
- gated: bfloat16 [256, 4096], P('ctx', 'chan')
All inputs are finite; a program needn't handle non-finite values.
Results may differ from a plain program's by a relative error of at most 0.0066.
Values may be sent and summed in bfloat16 or wider, within the bound.
A program may use at most 128 MiB of HBM per device.

v0:
```python
import jax
import jax.numpy as jnp
import numpy as np
from jax import lax
from jax.sharding import PartitionSpec as P


def split_pair(matrix):
    high = matrix.astype(jnp.bfloat16)
    low = (matrix - high.astype(np.float64)).astype(jnp.bfloat16)
    return (high, low)


def transforms(block):
    angle = np.pi * (np.arange(block)[:, None] + 0.5) * np.arange(block)[None, :] / block
    forward = np.concatenate([np.cos(angle), -np.sin(angle)], 0)
    inverse = np.concatenate([np.cos(angle), -np.sin(angle)], 0).T[::-1] / block
    sign = np.where(np.arange(block) % 2 == 0, 1.0, -1.0).astype(np.float32)
    return (split_pair(forward), split_pair(inverse), sign)


def times(a, b):
    return jnp.dot(a, b, preferred_element_type=jnp.float32)


def per_device(inputs, gain, w_in, w_out, history, filt_far, filt_near):
    chan_width = inputs.shape[1]
    block = filt_near.shape[0]
    ctx_index = lax.axis_index("ctx")
    ctx_count = lax.axis_size("ctx")
    column_count = chan_width // ctx_count
    (fwd_hi, fwd_lo), (inv_hi, inv_lo), sign = transforms(block)
    sign = jnp.asarray(sign)[None, :, None]
    gathered = lax.all_gather(inputs, "chan", axis=1, tiled=True)
    features = gathered.astype(jnp.float32)
    mean_sq = jnp.mean(features * features, axis=-1, keepdims=True)
    normed = (features * lax.rsqrt(mean_sq + 1e-06) * gain).astype(jnp.bfloat16)
    weights = w_in.transpose(1, 0, 2)
    fresh = [
        lax.all_to_all(
            times(normed, weights[i]).astype(jnp.bfloat16),
            "ctx",
            split_axis=1,
            concat_axis=0,
            tiled=True,
        )
        for i in range(3)
    ]
    value_cols, first_gate, second_gate = fresh
    hist_cols, far_cols = (
        lax.all_to_all(history, "ctx", split_axis=2, concat_axis=0, tiled=True),
        lax.all_to_all(filt_far, "ctx", split_axis=2, concat_axis=0, tiled=True),
    )
    near_cols = lax.dynamic_slice_in_dim(filt_near, ctx_index * column_count, column_count, 2)
    old_blocks = hist_cols.shape[0] // block

    def forward(rows):
        return times(fwd_hi, rows) + times(fwd_lo, rows)

    def as_columns(rows):
        count = rows.shape[0] // block
        return (
            rows.reshape(count, block, 2, column_count)
            .transpose(1, 2, 0, 3)
            .reshape(block, 2 * count * column_count)
        )

    def as_spectra(freq, count):
        return freq.reshape(2, block, 2, count, column_count).transpose(3, 0, 1, 2, 4)

    hist_f = as_spectra(forward(as_columns(hist_cols)), old_blocks)
    far_f = as_spectra(forward(as_columns(far_cols)), old_blocks)
    near_f = as_spectra(forward(as_columns(near_cols)), 1)
    filt_f = jnp.concatenate([far_f, near_f], 0)
    tap_re, tap_im = (filt_f[:, 0], filt_f[:, 1])
    turn = jnp.asarray(sign)[..., None]
    win_re = tap_re[:-1] + turn * tap_im[1:]
    win_im = tap_im[:-1] - turn * tap_re[1:]
    old_re, old_im = (hist_f[:, 0], hist_f[:, 1])
    sum_re = jnp.sum(win_re * old_re + win_im * old_im, 0)
    sum_im = jnp.sum(win_im * old_re - win_re * old_im, 0)

    def whole_conv(which, rows):
        new_f = forward(rows)
        new_re, new_im = (new_f[:block], new_f[block:])
        near_re, near_im = (near_f[0, 0, :, which], near_f[0, 1, :, which])
        total = jnp.concatenate(
            [
                sum_re[:, which] + near_re * new_re + near_im * new_im,
                sum_im[:, which] + near_im * new_re - near_re * new_im,
            ],
            0,
        )
        high = lax.reduce_precision(total, 8, 7)
        low = (total - high).astype(jnp.bfloat16)
        high = high.astype(jnp.bfloat16)
        return times(inv_hi, high) + times(inv_lo, high) + times(inv_hi, low)

    first_full = whole_conv(0, value_cols)
    gated_cols = (first_gate.astype(jnp.float32) * first_full).astype(jnp.bfloat16)
    second_full = whole_conv(1, gated_cols)
    mixed_cols = (second_gate.astype(jnp.float32) * second_full).astype(jnp.bfloat16)
    gated, mixed_in = (
        lax.all_to_all(gated_cols, "ctx", split_axis=0, concat_axis=1, tiled=True),
        lax.all_to_all(mixed_cols, "ctx", split_axis=0, concat_axis=1, tiled=True),
    )
    partial_out = jnp.dot(mixed_in, w_out, preferred_element_type=jnp.float32)
    mixed = lax.psum_scatter(partial_out, "chan", scatter_dimension=1, tiled=True).astype(
        jnp.bfloat16
    )
    return (mixed, gated)


def solution(mesh):
    placed = (
        P("ctx", "chan"),
        P(),
        P(None, None, "chan"),
        P("chan", None),
        P("ctx", None, "chan"),
        P("ctx", None, "chan"),
        P(None, None, "chan"),
    )
    return jax.shard_map(
        per_device,
        mesh=mesh,
        in_specs=placed,
        out_specs=(P("ctx", "chan"), P("ctx", "chan")),
        check_vma=False,
    )
```

profile of v0, /device:TPU:0, one launch (start us, length us, event | category | flops | bytes accessed | tf_op | source)
XLA Modules:
  0.0 149.4 jit_solution(18429281724813846505)
XLA Ops:
  7.2 16.0 %all_gather.3 = bf16[32,4096]{1,0:T(8,128)(2,1)S(1)} all-gather(bf16[32,1024]{1,0:T(8,128)(2,1)} %param.12), channel_id=1, replica_groups=mesh['ctx'=8,'chan'=4] {'chan'}, dimensions={1}, use_global_device_ids=true | all-gather | bytes 327680 | tf_op jit(solution)/shard_map/all_gather | solution.py:34
  23.4 5.0 %fusion.20 = bf16[4,8,8,128]{3,2,1,0:T(8,128)(2,1)S(1)} fusion(bf16[3,4096,1024]{2,1,0:T(8,128)(2,1)} %bitcast.211, bf16[32,4096]{1,0:T(8,128)(2,1)S(1)} %all_gather.3, f32[4096]{0:T(1024)} %param.13, f32[32]{0:T(128)S(1)} %add_rsqrt_fusion), kind=kOutput, calls=%fused_computation.40 | convolution fusion | flops 268992512 | bytes 8732800 | tf_op jit(solution)/shard_map/dot_general | solution.py:23
  29.0 3.7 %all-to-all-start.4 = ((bf16[32,8,128]{2,0,1:T(8,128)(2,1)}), bf16[32,8,128]{2,0,1:T(8,128)(2,1)S(1)}, u32[]{:S(2)}, u32[]{:S(2)}) async-start(bf16[32,8,128]{2,0,1:T(8,128)(2,1)} %bitcast.196), calls=%async_computation.4 | async-start | bytes 131072 | tf_op jit(solution)/shard_map/all_to_all | solution.py:40
  32.8 5.0 %fusion.21 = bf16[4,8,8,128]{3,2,1,0:T(8,128)(2,1)S(1)} fusion(bf16[3,4096,1024]{2,1,0:T(8,128)(2,1)} %bitcast.212, bf16[32,4096]{1,0:T(8,128)(2,1)S(1)} %all_gather.3, f32[4096]{0:T(1024)S(1)} %copy-done.15, f32[32]{0:T(128)S(1)} %add_rsqrt_fusion), kind=kOutput, calls=%fused_computation.41 | convolution fusion | flops 268992512 | bytes 8732800 | tf_op jit(solution)/shard_map/dot_general | solution.py:23
  38.4 4.2 %all-to-all-start.3 = ((bf16[32,8,128]{2,0,1:T(8,128)(2,1)}), bf16[32,8,128]{2,0,1:T(8,128)(2,1)S(1)}, u32[]{:S(2)}, u32[]{:S(2)}) async-start(bf16[32,8,128]{2,0,1:T(8,128)(2,1)} %bitcast.197), calls=%async_computation.3 | async-start | bytes 131072 | tf_op jit(solution)/shard_map/all_to_all | solution.py:40
  42.6 5.0 %fusion.22 = bf16[4,8,8,128]{3,2,1,0:T(8,128)(2,1)S(1)} fusion(bf16[3,4096,1024]{2,1,0:T(8,128)(2,1)} %bitcast.213, bf16[32,4096]{1,0:T(8,128)(2,1)S(1)} %all_gather.3, f32[4096]{0:T(1024)S(1)} %copy-done.15, f32[32]{0:T(128)S(1)} %add_rsqrt_fusion), kind=kOutput, calls=%fused_computation.42 | convolution fusion | flops 268992512 | bytes 8732800 | tf_op jit(solution)/shard_map/dot_general | solution.py:23
  48.2 4.2 %all-to-all-start = ((bf16[32,8,128]{2,0,1:T(8,128)(2,1)}), bf16[32,8,128]{2,0,1:T(8,128)(2,1)S(1)}, u32[]{:S(2)}, u32[]{:S(2)}) async-start(bf16[32,8,128]{2,0,1:T(8,128)(2,1)} %bitcast.198), calls=%async_computation | async-start | bytes 131072 | tf_op jit(solution)/shard_map/all_to_all | solution.py:40
  52.6 4.9 %copy.91 = bf16[256,2,1024]{0,1,2:T(2,128)(2,1)} copy(bf16[256,2,1024]{2,1,0:T(2,128)(2,1)} %param.17) | data formatting | bytes 2097152 | tf_op args[5]
  57.5 4.2 %all-to-all-start.1 = ((bf16[256,2,1024]{0,1,2:T(2,128)(2,1)}), bf16[256,2,1024]{0,1,2:T(2,128)(2,1)S(1)}, u32[]{:S(2)}, u32[]{:S(2)}) async-start(bf16[256,2,1024]{0,1,2:T(2,128)(2,1)} %copy.91), calls=%async_computation.1 | async-start | bytes 2097152 | tf_op jit(solution)/shard_map/all_to_all | solution.py:52
  63.1 4.9 %copy.94 = bf16[256,2,1024]{0,1,2:T(2,128)(2,1)} copy(bf16[256,2,1024]{2,1,0:T(2,128)(2,1)} %param.16) | data formatting | bytes 2097152 | tf_op args[4]
  68.0 1.2 fusion.58
  69.2 0.8 copy.105
  69.9 0.8 copy.108
  70.7 1.2 fusion.43
  71.9 5.1 %all-to-all-done.1 = bf16[256,2,1024]{0,1,2:T(2,128)(2,1)S(1)} async-done(((bf16[256,2,1024]{0,1,2:T(2,128)(2,1)}), bf16[256,2,1024]{0,1,2:T(2,128)(2,1)S(1)}, u32[]{:S(2)}, u32[]{:S(2)}) %all-to-all-start.1) | async-done | bytes 1048608 | tf_op jit(solution)/shard_map/all_to_all | solution.py:52
  77.0 3.6 %all-to-all-start.2 = ((bf16[256,2,1024]{0,1,2:T(2,128)(2,1)}), bf16[256,2,1024]{0,1,2:T(2,128)(2,1)S(1)}, u32[]{:S(2)}, u32[]{:S(2)}) async-start(bf16[256,2,1024]{0,1,2:T(2,128)(2,1)} %copy.94), calls=%async_computation.2 | async-start | bytes 2097152 | tf_op jit(solution)/shard_map/all_to_all | solution.py:51
  80.8 1.9 %fusion.10 = f32[512,128]{0,1:T(8,128)} fusion(f32[128,512]{1,0:T(8,128)S(1)} %fusion.43, bf16[512,256]{1,0:T(8,128)(2,1)} %constant.39, bf16[32,8,128]{2,0,1:T(8,128)(2,1)S(1)} %all-to-all-done.4), kind=kOutput, calls=%fused_computation.26 | convolution fusion | flops 33619968 | bytes 851968 | tf_op jit(solution)/shard_map/dot_general | solution.py:23
  82.8 0.7 fusion.61
  83.6 0.8 add_bitcast_fusion.1
  84.4 2.8 %copy.126 = f32[64,8,16,128]{3,2,1,0:T(8,128)} copy(f32[64,8,16,128]{3,1,2,0:T(8,128)S(1)} %add_bitcast_fusion.1) | data formatting | bytes 8388608
  87.2 8.7 %all-to-all-done.2 = bf16[256,2,1024]{0,1,2:T(2,128)(2,1)S(1)} async-done(((bf16[256,2,1024]{0,1,2:T(2,128)(2,1)}), bf16[256,2,1024]{0,1,2:T(2,128)(2,1)S(1)}, u32[]{:S(2)}, u32[]{:S(2)}) %all-to-all-start.2) | async-done | bytes 1048608 | tf_op jit(solution)/shard_map/all_to_all | solution.py:51
  96.0 0.7 fusion.62
  96.8 0.8 add_bitcast_fusion
  97.6 0.9 copy.128
  98.6 1.2 copy-done.2
  99.8 1.4 fusion.7
  101.3 1.8 %add_reduce_fusion = (f32[256,2,128]{2,1,0:T(2,128)S(1)}, f32[256,2,128]{2,1,0:T(2,128)S(1)}) fusion(f32[8,256,2,128]{3,0,2,1:T(8,128)S(1)} %get-tuple-element.5, f32[8,256,2,128]{3,0,2,1:T(8,128)S(1)} %get-tuple-element.4, f32[8,2,256,2,128]{4,0,3,2,1:T(8,128)S(1)} %bitcast.200), kind=kLoop, calls=%fused_computation.20 | loop fusion | flops 4063232 | bytes 8912896 | tf_op jit(solution)/shard_map/reduce_sum | solution.py:80
  106.2 7.4 %all_to_all.101 = bf16[8,32,128]{2,1,0:T(8,128)(2,1)S(1)} all-to-all(bf16[8,32,128]{2,1,0:T(8,128)(2,1)S(1)} %bitcast.209), channel_id=1, replica_groups=mesh['ctx'=8,'chan'=4] {'ctx'}, dimensions={0} | all-to-all | bytes 131072 | tf_op jit(solution)/shard_map/all_to_all | solution.py:105
  113.6 5.8 %fusion.39 = f32[32,4096]{1,0:T(8,128)} fusion(bf16[1024,4096]{1,0:T(8,128)(2,1)} %param.15, bf16[8,32,128]{2,1,0:T(8,128)(2,1)S(1)} %all_to_all.101), kind=kOutput, calls=%fused_computation.74 | convolution fusion | flops 268435456 | bytes 8978432 | tf_op jit(solution)/shard_map/dot_general | solution.py:107
  119.5 7.4 %all_to_all.102 = bf16[8,32,128]{2,1,0:T(8,128)(2,1)S(1)} all-to-all(bf16[8,32,128]{2,1,0:T(8,128)(2,1)S(1)} %bitcast.210), channel_id=1, replica_groups=mesh['ctx'=8,'chan'=4] {'ctx'}, dimensions={0} | all-to-all | bytes 131072 | tf_op jit(solution)/shard_map/all_to_all | solution.py:104
  127.6 13.5 %reduce-scatter.2.cloned.1.call-done = f32[32,1024]{1,0:T(8,128)} async-done(((f32[32,4096]{1,0:T(8,128)}), f32[32,1024]{1,0:T(8,128)}) %reduce-scatter.2.cloned.1.call-update) | async-done | bytes 131088 | tf_op jit(solution)/shard_map/reduce_scatter | solution.py:108
  141.0 1.5 %convert_element_type.71 = bf16[32,1024]{1,0:T(8,128)(2,1)} convert(f32[32,1024]{1,0:T(8,128)} %reduce-scatter.2.cloned.1.call-done) | non-fusion elementwise | flops 32768 | bytes 196608 | tf_op jit(solution)/shard_map/convert_element_type | solution.py:108
  (68 shorter events, 7.8 us)
Async XLA Ops:
  7.2 45.3 %copy-start = (bf16[256,2,1024]{2,1,0:T(2,128)(2,1)S(1)}, bf16[256,2,1024]{2,1,0:T(2,128)(2,1)}, u32[]{:S(2)}) copy-start(bf16[256,2,1024]{2,1,0:T(2,128)(2,1)} %param.18) | copy-start | bytes 3145732
  23.4 9.4 %copy-start.15 = (f32[4096]{0:T(1024)S(1)}, f32[4096]{0:T(1024)}, u32[]{:S(2)}) copy-start(f32[4096]{0:T(1024)} %param.13) | copy-start | bytes 49156
  29.0 9.4 %all-to-all-start.4 = ((bf16[32,8,128]{2,0,1:T(8,128)(2,1)}), bf16[32,8,128]{2,0,1:T(8,128)(2,1)S(1)}, u32[]{:S(2)}, u32[]{:S(2)}) async-start(bf16[32,8,128]{2,0,1:T(8,128)(2,1)} %bitcast.196), calls=%async_computation.4 | async-start | bytes 131072 | tf_op jit(solution)/shard_map/all_to_all | solution.py:40
  38.4 9.8 %all-to-all-start.3 = ((bf16[32,8,128]{2,0,1:T(8,128)(2,1)}), bf16[32,8,128]{2,0,1:T(8,128)(2,1)S(1)}, u32[]{:S(2)}, u32[]{:S(2)}) async-start(bf16[32,8,128]{2,0,1:T(8,128)(2,1)} %bitcast.197), calls=%async_computation.3 | async-start | bytes 131072 | tf_op jit(solution)/shard_map/all_to_all | solution.py:40
  47.6 14.1 %copy-start.5 = (bf16[512,256]{1,0:T(8,128)(2,1)S(1)}, bf16[512,256]{1,0:T(8,128)(2,1)}, u32[]{:S(2)}) copy-start(bf16[512,256]{1,0:T(8,128)(2,1)} %constant.30.clone) | copy-start | bytes 786436
  47.6 14.3 %copy-start.3 = (bf16[512,256]{1,0:T(8,128)(2,1)S(1)}, bf16[512,256]{1,0:T(8,128)(2,1)}, u32[]{:S(2)}) copy-start(bf16[512,256]{1,0:T(8,128)(2,1)} %constant.31.clone) | copy-start | bytes 786436
  48.2 9.2 %all-to-all-start = ((bf16[32,8,128]{2,0,1:T(8,128)(2,1)}), bf16[32,8,128]{2,0,1:T(8,128)(2,1)S(1)}, u32[]{:S(2)}, u32[]{:S(2)}) async-start(bf16[32,8,128]{2,0,1:T(8,128)(2,1)} %bitcast.198), calls=%async_computation | async-start | bytes 131072 | tf_op jit(solution)/shard_map/all_to_all | solution.py:40
  57.5 19.6 %all-to-all-start.1 = ((bf16[256,2,1024]{0,1,2:T(2,128)(2,1)}), bf16[256,2,1024]{0,1,2:T(2,128)(2,1)S(1)}, u32[]{:S(2)}, u32[]{:S(2)}) async-start(bf16[256,2,1024]{0,1,2:T(2,128)(2,1)} %copy.91), calls=%async_computation.1 | async-start | bytes 2097152 | tf_op jit(solution)/shard_map/all_to_all | solution.py:52
  77.0 18.9 %all-to-all-start.2 = ((bf16[256,2,1024]{0,1,2:T(2,128)(2,1)}), bf16[256,2,1024]{0,1,2:T(2,128)(2,1)S(1)}, u32[]{:S(2)}, u32[]{:S(2)}) async-start(bf16[256,2,1024]{0,1,2:T(2,128)(2,1)} %copy.94), calls=%async_computation.2 | async-start | bytes 2097152 | tf_op jit(solution)/shard_map/all_to_all | solution.py:51
  80.6 60.5 %reduce-scatter.2.cloned.1.call-start = ((), (), s32[]{:S(2)}) async-start(), calls=%async_computation.8 | async-start | bytes 655360 | tf_op jit(solution)/shard_map/reduce_scatter | solution.py:108
  97.6 2.2 %copy-start.2 = (f32[64,8,16,128]{3,2,1,0:T(8,128)S(1)}, f32[64,8,16,128]{3,2,1,0:T(8,128)}, u32[]{:S(2)}) copy-start(f32[64,8,16,128]{3,2,1,0:T(8,128)} %copy.126) | copy-start | bytes 12582916
  97.6 2.2 %copy-start.14 = (f32[256]{0:T(256)S(1)}, f32[256]{0:T(256)}, u32[]{:S(2)}) copy-start(f32[256]{0:T(256)} %constant.29.clone) | copy-start | bytes 3076
  101.3 2.5 %copy-start.7 = (f32[512,128]{0,1:T(8,128)S(1)}, f32[512,128]{0,1:T(8,128)}, u32[]{:S(2)}) copy-start(f32[512,128]{0,1:T(8,128)} %fusion.10) | copy-start | bytes 786436
  101.3 2.5 %copy-start.12 = (f32[1,1,256,1,128]{2,1,4,3,0:T(1,128)S(1)}, f32[1,1,256,1,128]{2,1,4,3,0:T(1,128)}, u32[]{:S(2)}) copy-start(f32[1,1,256,1,128]{2,1,4,3,0:T(1,128)} %get-tuple-element.10) | copy-start | bytes 393220
  101.3 2.5 %copy-start.13 = (f32[1,1,256,1,128]{2,1,4,3,0:T(1,128)S(1)}, f32[1,1,256,1,128]{2,1,4,3,0:T(1,128)}, u32[]{:S(2)}) copy-start(f32[1,1,256,1,128]{2,1,4,3,0:T(1,128)} %get-tuple-element.11) | copy-start | bytes 393220
  101.3 2.6 %copy-start.4 = (bf16[256,512]{1,0:T(8,128)(2,1)S(1)}, bf16[256,512]{1,0:T(8,128)(2,1)}, u32[]{:S(2)}) copy-start(bf16[256,512]{1,0:T(8,128)(2,1)} %constant.32.clone) | copy-start | bytes 786436
  101.3 2.8 %copy-start.6 = (bf16[256,512]{1,0:T(8,128)(2,1)S(1)}, bf16[256,512]{1,0:T(8,128)(2,1)}, u32[]{:S(2)}) copy-start(bf16[256,512]{1,0:T(8,128)(2,1)} %constant.33.clone) | copy-start | bytes 786436
  101.3 3.0 %copy-start.9 = (f32[256,128]{0,1:T(8,128)S(1)}, f32[256,128]{0,1:T(8,128)}, u32[]{:S(2)}) copy-start(f32[256,128]{0,1:T(8,128)} %copy.105) | copy-start | bytes 393220
  103.1 2.1 %copy-start.10 = (f32[1,1,256,1,128]{2,1,4,3,0:T(1,128)S(1)}, f32[1,1,256,1,128]{2,1,4,3,0:T(1,128)}, u32[]{:S(2)}) copy-start(f32[1,1,256,1,128]{2,1,4,3,0:T(1,128)} %get-tuple-element.12) | copy-start | bytes 393220
  103.1 2.1 %copy-start.11 = (f32[1,1,256,1,128]{2,1,4,3,0:T(1,128)S(1)}, f32[1,1,256,1,128]{2,1,4,3,0:T(1,128)}, u32[]{:S(2)}) copy-start(f32[1,1,256,1,128]{2,1,4,3,0:T(1,128)} %get-tuple-element.13) | copy-start | bytes 393220
  103.6 2.2 %copy-start.8 = (f32[256,128]{0,1:T(8,128)S(1)}, f32[256,128]{0,1:T(8,128)}, u32[]{:S(2)}) copy-start(f32[256,128]{0,1:T(8,128)} %copy.108) | copy-start | bytes 393220
  113.6 29.0 %copy-start.1 = (bf16[256,2,1024]{2,1,0:T(2,128)(2,1)S(1)}, bf16[256,2,1024]{2,1,0:T(2,128)(2,1)}, u32[]{:S(2)}) copy-start(bf16[256,2,1024]{2,1,0:T(2,128)(2,1)} %param.18) | copy-start | bytes 3145732
Sparse Core Ops, SparseCore 0:
  119.5 21.4 reduce-scatter.1
where the time goes:
time: 150 us; the launch traced here: 149 us
  blocking collectives  30.8 us (21%)
  matrix products  29.2 us (19%)
  waiting for transfers between devices  27.4 us (18%)
  local copies, waits for them, and re-layouts  22.4 us (15%)
  starting transfers between devices  20.1 us (13%)
  between operations  14.5 us (10%)
  other arithmetic  5.08 us (3%)
    dot_general x19, matrix products, times(): return jnp.dot(a, b, preferred_element_type=jnp.float32)  23.4 us
    all_gather x1, blocking collectives, per_device(): gathered = lax.all_gather(inputs, 'chan', axis=1, tiled=True)  16 us
    unnamed x40, local copies, waits for them, and re-layouts  15.3 us
    reduce_scatter x1, waiting for transfers between devices, per_device(): lax.psum_scatter(partial_out, 'chan', scatter_dimension=1, tiled=True)  13.5 us
    all_to_all x3, starting transfers between devices, per_device(): lax.all_to_all(times(normed, weights[i]).astype(jnp.bfloat16), 'ctx', spl...  12.1 us
    all_to_all x1, waiting for transfers between devices, per_device(): lax.all_to_all(history, 'ctx', split_axis=2, concat_axis=0, tiled=True)  8.69 us
    all_to_all x1, blocking collectives, per_device(): lax.all_to_all(gated_cols, 'ctx', split_axis=0, concat_axis=1, tiled=True)  7.4 us
    all_to_all x1, blocking collectives, per_device(): lax.all_to_all(mixed_cols, 'ctx', split_axis=0, concat_axis=1, tiled=True)  7.4 us
  transfers between devices with their start and end apart: 6, of which 3 were waited for; matrix products, arithmetic and copies ran while one was open for 22% of the time, Pallas kernels for 0%

commit v1 on v0

--- a/solution.py
+++ b/solution.py
@@ -3,6 +3,12 @@
 import numpy as np
 from jax import lax
 from jax.sharding import PartitionSpec as P
+
+
+def stacked_exchange(x, axis, split, join):
+    pieces = jnp.split(x, lax.axis_size(axis), axis=split)
+    got = lax.all_to_all(jnp.stack(pieces), axis, 0, 0)
+    return jnp.concatenate(got, axis=join)
 
 
 def split_pair(matrix):
@@ -37,13 +43,7 @@
     normed = (features * lax.rsqrt(mean_sq + 1e-06) * gain).astype(jnp.bfloat16)
     weights = w_in.transpose(1, 0, 2)
     fresh = [
-        lax.all_to_all(
-            times(normed, weights[i]).astype(jnp.bfloat16),
-            "ctx",
-            split_axis=1,
-            concat_axis=0,
-            tiled=True,
-        )
+        stacked_exchange(times(normed, weights[i]).astype(jnp.bfloat16), "ctx", 1, 0)
         for i in range(3)
     ]
     value_cols, first_gate, second_gate = fresh

time: 150 us -> 173 us (1.15)
  waiting for transfers between devices: 27.4 us -> 40 us
  local copies, waits for them, and re-layouts: 22.4 us -> 34.9 us
  matrix products: 29.2 us -> 27.4 us
    unnamed x40 -> x61, local copies, waits for them, and re-layouts: 15.3 us -> 27.9 us
    all_to_all x1, waiting for transfers between devices: 5.15 us -> 12.4 us  [per_device(): lax.all_to_all(filt_far, 'ctx', split_axis=2, concat_axis=0, tiled=True)]
    all_to_all x3, waiting for transfers between devices: 0.02 us -> 4.42 us  [stacked_exchange(): got = lax.all_to_all(jnp.stack(pieces), axis, 0, 0)]
    all_to_all x3 -> x0, local copies, waits for them, and re-layouts: 1.94 us -> none  [per_device(): lax.all_to_all(times(normed, weights[i]).astype(jnp.bfloat16), 'ctx', spl...]
    dot_general x19, matrix products: 23.4 us -> 21.6 us  [times(): return jnp.dot(a, b, preferred_element_type=jnp.float32)]
    another operation x0 -> x3, local copies, waits for them, and re-layouts: none -> 1.81 us  [stacked_exchange(): got = lax.all_to_all(jnp.stack(pieces), axis, 0, 0)]
  transfers between devices with their start and end apart: 6 -> 6, of which waited for: 3 -> 4; matrix products, arithmetic and copies ran while one was open for 22% -> 23% of each run, Pallas kernels for 0% -> 0%
where the time goes in v1:
time: 173 us; the launch traced here: 172 us
  waiting for transfers between devices  40 us (23%)
  local copies, waits for them, and re-layouts  34.9 us (20%)
  blocking collectives  30.8 us (18%)
  matrix products  27.4 us (16%)
  starting transfers between devices  19.2 us (11%)
  between operations  14.5 us (8%)
  other arithmetic  5.09 us (3%)
    unnamed x61, local copies, waits for them, and re-layouts  27.9 us
    dot_general x19, matrix products, times(): return jnp.dot(a, b, preferred_element_type=jnp.float32)  21.6 us
    all_gather x1, blocking collectives, per_device(): gathered = lax.all_gather(inputs, 'chan', axis=1, tiled=True)  16 us
    reduce_scatter x1, waiting for transfers between devices, per_device(): lax.psum_scatter(partial_out, 'chan', scatter_dimension=1, tiled=True)  13.5 us
    all_to_all x1, waiting for transfers between devices, per_device(): lax.all_to_all(filt_far, 'ctx', split_axis=2, concat_axis=0, tiled=True)  12.4 us
    all_to_all x3, starting transfers between devices, stacked_exchange(): got = lax.all_to_all(jnp.stack(pieces), axis, 0, 0)  11.3 us
    all_to_all x1, waiting for transfers between devices, per_device(): lax.all_to_all(history, 'ctx', split_axis=2, concat_axis=0, tiled=True)  9.65 us
    all_to_all x1, blocking collectives, per_device(): lax.all_to_all(mixed_cols, 'ctx', split_axis=0, concat_axis=1, tiled=True)  7.4 us
  transfers between devices with their start and end apart: 6, of which 4 were waited for; matrix products, arithmetic and copies ran while one was open for 23% of the time, Pallas kernels for 0%

profile of v1, /device:TPU:0, one launch (start us, length us, event | category | flops | bytes accessed | tf_op | source)
XLA Modules:
  0.0 171.8 jit_solution(15905970792522516353)
XLA Ops:
  7.2 16.0 %all_gather.3 = bf16[32,4096]{1,0:T(8,128)(2,1)S(1)} all-gather(bf16[32,1024]{1,0:T(8,128)(2,1)} %param.12), channel_id=1, replica_groups=mesh['ctx'=8,'chan'=4] {'chan'}, dimensions={1}, use_global_device_ids=true | all-gather | bytes 327680 | tf_op jit(solution)/shard_map/all_gather | solution.py:40
  23.4 5.0 %fusion.17 = bf16[32,1024]{1,0:T(8,128)(2,1)S(1)} fusion(bf16[3,4096,1024]{2,1,0:T(8,128)(2,1)} %bitcast.284, bf16[32,4096]{1,0:T(8,128)(2,1)S(1)} %all_gather.3, f32[4096]{0:T(1024)} %param.13, f32[32]{0:T(128)S(1)} %add_rsqrt_fusion), kind=kOutput, calls=%fused_computation.37 | convolution fusion | flops 268992512 | bytes 8732800 | tf_op jit(solution)/shard_map/dot_general | solution.py:29
  33.2 3.7 %all-to-all-start = ((bf16[8,32,128]{2,1,0:T(8,128)(2,1)}), bf16[8,32,128]{2,1,0:T(8,128)(2,1)S(1)}, u32[]{:S(2)}, u32[]{:S(2)}) async-start(bf16[8,32,128]{2,1,0:T(8,128)(2,1)} %constant_dynamic-update-slice_fusion), calls=%async_computation | async-start | bytes 131072 | tf_op jit(solution)/shard_map/all_to_all | solution.py:10
  36.9 5.0 %fusion.18 = bf16[32,1024]{1,0:T(8,128)(2,1)S(1)} fusion(bf16[3,4096,1024]{2,1,0:T(8,128)(2,1)} %bitcast.285, bf16[32,4096]{1,0:T(8,128)(2,1)S(1)} %all_gather.3, f32[4096]{0:T(1024)S(1)} %copy-done.15, f32[32]{0:T(128)S(1)} %add_rsqrt_fusion), kind=kOutput, calls=%fused_computation.38 | convolution fusion | flops 268992512 | bytes 8732800 | tf_op jit(solution)/shard_map/dot_general | solution.py:29
  41.9 5.0 %fusion.19 = bf16[32,1024]{1,0:T(8,128)(2,1)S(1)} fusion(bf16[3,4096,1024]{2,1,0:T(8,128)(2,1)} %bitcast.286, bf16[32,4096]{1,0:T(8,128)(2,1)S(1)} %all_gather.3, f32[4096]{0:T(1024)S(1)} %copy-done.15, f32[32]{0:T(128)S(1)} %add_rsqrt_fusion), kind=kOutput, calls=%fused_computation.39 | convolution fusion | flops 268992512 | bytes 8732800 | tf_op jit(solution)/shard_map/dot_general | solution.py:29
  56.4 4.2 %all-to-all-start.3 = ((bf16[8,32,128]{2,1,0:T(8,128)(2,1)}), bf16[8,32,128]{2,1,0:T(8,128)(2,1)S(1)}, u32[]{:S(2)}, u32[]{:S(2)}) async-start(bf16[8,32,128]{2,1,0:T(8,128)(2,1)} %constant_dynamic-update-slice_fusion.8), calls=%async_computation.3 | async-start | bytes 131072 | tf_op jit(solution)/shard_map/all_to_all | solution.py:10
  61.2 4.4 %all-to-all-done.3 = bf16[8,32,128]{2,1,0:T(8,128)(2,1)S(1)} async-done(((bf16[8,32,128]{2,1,0:T(8,128)(2,1)}), bf16[8,32,128]{2,1,0:T(8,128)(2,1)S(1)}, u32[]{:S(2)}, u32[]{:S(2)}) %all-to-all-start.3) | async-done | bytes 65568 | tf_op jit(solution)/shard_map/all_to_all | solution.py:10
  65.6 3.3 %all-to-all-start.4 = ((bf16[8,32,128]{2,1,0:T(8,128)(2,1)}), bf16[8,32,128]{2,1,0:T(8,128)(2,1)S(1)}, u32[]{:S(2)}, u32[]{:S(2)}) async-start(bf16[8,32,128]{2,1,0:T(8,128)(2,1)} %constant_dynamic-update-slice_fusion.16), calls=%async_computation.4 | async-start | bytes 131072 | tf_op jit(solution)/shard_map/all_to_all | solution.py:10
  70.1 4.9 %copy.79 = bf16[256,2,1024]{0,1,2:T(2,128)(2,1)} copy(bf16[256,2,1024]{2,1,0:T(2,128)(2,1)} %param.17) | data formatting | bytes 2097152 | tf_op args[5]
  75.0 4.9 %copy.82 = bf16[256,2,1024]{0,1,2:T(2,128)(2,1)} copy(bf16[256,2,1024]{2,1,0:T(2,128)(2,1)} %param.16) | data formatting | bytes 2097152 | tf_op args[4]
  79.9 4.1 %all-to-all-start.1 = ((bf16[256,2,1024]{0,1,2:T(2,128)(2,1)}), bf16[256,2,1024]{0,1,2:T(2,128)(2,1)S(1)}, u32[]{:S(2)}, u32[]{:S(2)}) async-start(bf16[256,2,1024]{0,1,2:T(2,128)(2,1)} %copy.79), calls=%async_computation.1 | async-start | bytes 2097152 | tf_op jit(solution)/shard_map/all_to_all | solution.py:52
  84.0 1.2 fusion.50
  85.2 0.8 copy.93
  86.0 0.8 copy.90
  87.0 12.4 %all-to-all-done.1 = bf16[256,2,1024]{0,1,2:T(2,128)(2,1)S(1)} async-done(((bf16[256,2,1024]{0,1,2:T(2,128)(2,1)}), bf16[256,2,1024]{0,1,2:T(2,128)(2,1)S(1)}, u32[]{:S(2)}, u32[]{:S(2)}) %all-to-all-start.1) | async-done | bytes 1048608 | tf_op jit(solution)/shard_map/all_to_all | solution.py:52
  99.4 3.6 %all-to-all-start.2 = ((bf16[256,2,1024]{0,1,2:T(2,128)(2,1)}), bf16[256,2,1024]{0,1,2:T(2,128)(2,1)S(1)}, u32[]{:S(2)}, u32[]{:S(2)}) async-start(bf16[256,2,1024]{0,1,2:T(2,128)(2,1)} %copy.82), calls=%async_computation.2 | async-start | bytes 2097152 | tf_op jit(solution)/shard_map/all_to_all | solution.py:51
  103.2 0.9 fusion.10
  104.3 0.7 fusion.53
  105.0 0.8 add_bitcast_fusion.1
  105.8 2.8 %copy.108 = f32[64,8,16,128]{3,2,1,0:T(8,128)} copy(f32[64,8,16,128]{3,1,2,0:T(8,128)S(1)} %add_bitcast_fusion.1) | data formatting | bytes 8388608
  108.6 9.6 %all-to-all-done.2 = bf16[256,2,1024]{0,1,2:T(2,128)(2,1)S(1)} async-done(((bf16[256,2,1024]{0,1,2:T(2,128)(2,1)}), bf16[256,2,1024]{0,1,2:T(2,128)(2,1)S(1)}, u32[]{:S(2)}, u32[]{:S(2)}) %all-to-all-start.2) | async-done | bytes 1048608 | tf_op jit(solution)/shard_map/all_to_all | solution.py:51
  118.4 0.7 fusion.54
  119.2 0.8 add_bitcast_fusion
  120.0 0.9 copy.110
  121.0 1.2 copy-done.2
  122.2 1.4 fusion.7
  123.7 1.8 %add_reduce_fusion = (f32[256,2,128]{2,1,0:T(2,128)S(1)}, f32[256,2,128]{2,1,0:T(2,128)S(1)}) fusion(f32[8,256,2,128]{3,0,2,1:T(8,128)S(1)} %get-tuple-element.5, f32[8,256,2,128]{3,0,2,1:T(8,128)S(1)} %get-tuple-element.4, f32[8,2,256,2,128]{4,0,3,2,1:T(8,128)S(1)} %bitcast.273), kind=kLoop, calls=%fused_computation.20 | loop fusion | flops 4063232 | bytes 8912896 | tf_op jit(solution)/shard_map/reduce_sum | solution.py:80
  128.5 7.4 %all_to_all.71 = bf16[8,32,128]{2,1,0:T(8,128)(2,1)S(1)} all-to-all(bf16[8,32,128]{2,1,0:T(8,128)(2,1)S(1)} %bitcast.282), channel_id=1, replica_groups=mesh['ctx'=8,'chan'=4] {'ctx'}, dimensions={0} | all-to-all | bytes 131072 | tf_op jit(solution)/shard_map/all_to_all | solution.py:105
  135.9 5.8 %fusion.36 = f32[32,4096]{1,0:T(8,128)} fusion(bf16[1024,4096]{1,0:T(8,128)(2,1)} %param.15, bf16[8,32,128]{2,1,0:T(8,128)(2,1)S(1)} %all_to_all.71), kind=kOutput, calls=%fused_computation.71 | convolution fusion | flops 268435456 | bytes 8978432 | tf_op jit(solution)/shard_map/dot_general | solution.py:107
  141.9 7.4 %all_to_all.72 = bf16[8,32,128]{2,1,0:T(8,128)(2,1)S(1)} all-to-all(bf16[8,32,128]{2,1,0:T(8,128)(2,1)S(1)} %bitcast.283), channel_id=1, replica_groups=mesh['ctx'=8,'chan'=4] {'ctx'}, dimensions={0} | all-to-all | bytes 131072 | tf_op jit(solution)/shard_map/all_to_all | solution.py:104
  149.9 13.5 %reduce-scatter.2.cloned.1.call-done = f32[32,1024]{1,0:T(8,128)} async-done(((f32[32,4096]{1,0:T(8,128)}), f32[32,1024]{1,0:T(8,128)}) %reduce-scatter.2.cloned.1.call-update) | async-done | bytes 131088 | tf_op jit(solution)/shard_map/reduce_scatter | solution.py:108
  163.5 1.5 convert_element_type.63
  (89 shorter events, 20.5 us)
Async XLA Ops:
  7.2 48.2 %copy-start = (bf16[256,2,1024]{2,1,0:T(2,128)(2,1)S(1)}, bf16[256,2,1024]{2,1,0:T(2,128)(2,1)}, u32[]{:S(2)}) copy-start(bf16[256,2,1024]{2,1,0:T(2,128)(2,1)} %param.18) | copy-start | bytes 3145732
  23.4 13.6 %copy-start.15 = (f32[4096]{0:T(1024)S(1)}, f32[4096]{0:T(1024)}, u32[]{:S(2)}) copy-start(f32[4096]{0:T(1024)} %param.13) | copy-start | bytes 49156
  33.2 23.2 %all-to-all-start = ((bf16[8,32,128]{2,1,0:T(8,128)(2,1)}), bf16[8,32,128]{2,1,0:T(8,128)(2,1)S(1)}, u32[]{:S(2)}, u32[]{:S(2)}) async-start(bf16[8,32,128]{2,1,0:T(8,128)(2,1)} %constant_dynamic-update-slice_fusion), calls=%async_computation | async-start | bytes 131072 | tf_op jit(solution)/shard_map/all_to_all | solution.py:10
  41.9 13.6 %copy-start.4 = (bf16[512,256]{1,0:T(8,128)(2,1)S(1)}, bf16[512,256]{1,0:T(8,128)(2,1)}, u32[]{:S(2)}) copy-start(bf16[512,256]{1,0:T(8,128)(2,1)} %constant.30.clone) | copy-start | bytes 786436
  41.9 27.0 %copy-start.3 = (bf16[512,256]{1,0:T(8,128)(2,1)S(1)}, bf16[512,256]{1,0:T(8,128)(2,1)}, u32[]{:S(2)}) copy-start(bf16[512,256]{1,0:T(8,128)(2,1)} %constant.31.clone) | copy-start | bytes 786436
  56.4 9.2 %all-to-all-start.3 = ((bf16[8,32,128]{2,1,0:T(8,128)(2,1)}), bf16[8,32,128]{2,1,0:T(8,128)(2,1)S(1)}, u32[]{:S(2)}, u32[]{:S(2)}) async-start(bf16[8,32,128]{2,1,0:T(8,128)(2,1)} %constant_dynamic-update-slice_fusion.8), calls=%async_computation.3 | async-start | bytes 131072 | tf_op jit(solution)/shard_map/all_to_all | solution.py:10
  65.6 14.3 %all-to-all-start.4 = ((bf16[8,32,128]{2,1,0:T(8,128)(2,1)}), bf16[8,32,128]{2,1,0:T(8,128)(2,1)S(1)}, u32[]{:S(2)}, u32[]{:S(2)}) async-start(bf16[8,32,128]{2,1,0:T(8,128)(2,1)} %constant_dynamic-update-slice_fusion.16), calls=%async_computation.4 | async-start | bytes 131072 | tf_op jit(solution)/shard_map/all_to_all | solution.py:10
  79.9 19.5 %all-to-all-start.1 = ((bf16[256,2,1024]{0,1,2:T(2,128)(2,1)}), bf16[256,2,1024]{0,1,2:T(2,128)(2,1)S(1)}, u32[]{:S(2)}, u32[]{:S(2)}) async-start(bf16[256,2,1024]{0,1,2:T(2,128)(2,1)} %copy.79), calls=%async_computation.1 | async-start | bytes 2097152 | tf_op jit(solution)/shard_map/all_to_all | solution.py:52
  99.4 18.9 %all-to-all-start.2 = ((bf16[256,2,1024]{0,1,2:T(2,128)(2,1)}), bf16[256,2,1024]{0,1,2:T(2,128)(2,1)S(1)}, u32[]{:S(2)}, u32[]{:S(2)}) async-start(bf16[256,2,1024]{0,1,2:T(2,128)(2,1)} %copy.82), calls=%async_computation.2 | async-start | bytes 2097152 | tf_op jit(solution)/shard_map/all_to_all | solution.py:51
  103.0 60.5 %reduce-scatter.2.cloned.1.call-start = ((), (), s32[]{:S(2)}) async-start(), calls=%async_computation.8 | async-start | bytes 655360 | tf_op jit(solution)/shard_map/reduce_scatter | solution.py:108
  120.0 2.2 %copy-start.2 = (f32[64,8,16,128]{3,2,1,0:T(8,128)S(1)}, f32[64,8,16,128]{3,2,1,0:T(8,128)}, u32[]{:S(2)}) copy-start(f32[64,8,16,128]{3,2,1,0:T(8,128)} %copy.108) | copy-start | bytes 12582916
  120.0 2.2 %copy-start.14 = (f32[256]{0:T(256)S(1)}, f32[256]{0:T(256)}, u32[]{:S(2)}) copy-start(f32[256]{0:T(256)} %constant.29.clone) | copy-start | bytes 3076
  123.6 2.6 %copy-start.7 = (f32[512,128]{0,1:T(8,128)S(1)}, f32[512,128]{0,1:T(8,128)}, u32[]{:S(2)}) copy-start(f32[512,128]{0,1:T(8,128)} %fusion.10) | copy-start | bytes 786436
  123.7 2.6 %copy-start.12 = (f32[1,1,256,1,128]{2,1,4,3,0:T(1,128)S(1)}, f32[1,1,256,1,128]{2,1,4,3,0:T(1,128)}, u32[]{:S(2)}) copy-start(f32[1,1,256,1,128]{2,1,4,3,0:T(1,128)} %get-tuple-element.10) | copy-start | bytes 393220
  123.7 2.6 %copy-start.13 = (f32[1,1,256,1,128]{2,1,4,3,0:T(1,128)S(1)}, f32[1,1,256,1,128]{2,1,4,3,0:T(1,128)}, u32[]{:S(2)}) copy-start(f32[1,1,256,1,128]{2,1,4,3,0:T(1,128)} %get-tuple-element.11) | copy-start | bytes 393220
  123.7 2.7 %copy-start.5 = (bf16[256,512]{1,0:T(8,128)(2,1)S(1)}, bf16[256,512]{1,0:T(8,128)(2,1)}, u32[]{:S(2)}) copy-start(bf16[256,512]{1,0:T(8,128)(2,1)} %constant.32.clone) | copy-start | bytes 786436
  123.7 2.9 %copy-start.6 = (bf16[256,512]{1,0:T(8,128)(2,1)S(1)}, bf16[256,512]{1,0:T(8,128)(2,1)}, u32[]{:S(2)}) copy-start(bf16[256,512]{1,0:T(8,128)(2,1)} %constant.33.clone) | copy-start | bytes 786436
  125.5 1.3 copy-start.9
  125.5 2.1 %copy-start.10 = (f32[1,1,256,1,128]{2,1,4,3,0:T(1,128)S(1)}, f32[1,1,256,1,128]{2,1,4,3,0:T(1,128)}, u32[]{:S(2)}) copy-start(f32[1,1,256,1,128]{2,1,4,3,0:T(1,128)} %get-tuple-element.12) | copy-start | bytes 393220
  125.5 2.1 %copy-start.11 = (f32[1,1,256,1,128]{2,1,4,3,0:T(1,128)S(1)}, f32[1,1,256,1,128]{2,1,4,3,0:T(1,128)}, u32[]{:S(2)}) copy-start(f32[1,1,256,1,128]{2,1,4,3,0:T(1,128)} %get-tuple-element.13) | copy-start | bytes 393220
  125.9 2.2 %copy-start.8 = (f32[256,128]{0,1:T(8,128)S(1)}, f32[256,128]{0,1:T(8,128)}, u32[]{:S(2)}) copy-start(f32[256,128]{0,1:T(8,128)} %copy.93) | copy-start | bytes 393220
  135.9 29.1 %copy-start.1 = (bf16[256,2,1024]{2,1,0:T(2,128)(2,1)S(1)}, bf16[256,2,1024]{2,1,0:T(2,128)(2,1)}, u32[]{:S(2)}) copy-start(bf16[256,2,1024]{2,1,0:T(2,128)(2,1)} %param.18) | copy-start | bytes 3145732
Sparse Core Ops, SparseCore 0:
  141.9 21.5 reduce-scatter.1
